TPU v7x, 32 devices: a whole 2x2x4 slice. The times are simulated.
32 devices in a mesh: req: 16 (over z, x, core), tp: 2 (over y).
Axes of the slice: x: 2, y: 2, z: 4, core: 2. Of those that a mesh axis runs over, the one named last changes fastest.
Arguments:
- state: bfloat16 [256, 2048], P('req'), may hold values from -3 to 3
- norm_gain: float32 [2048], replicated, may hold values from 0.25 to 4
- w_qkv: bfloat16 [2048, 2, 512], P(None, 'tp'), may hold values from -0.125 to 0.125
- w_out: bfloat16 [2, 256, 2048], P('tp'), may hold values from -0.25 to 0.25
- kv_cache: bfloat16 [2944, 2, 16, 256], P('req', 'tp')
- lengths: int32 [256], P('req'), may hold values from 32 to 1024, as said below
- page_table: int32 [256, 64], P('req'), may hold values from 0 to 183, as said below
- dest_slot: int32 [256], P('req'), may hold values from 0 to 255, as said below
Outputs:
- new_state: bfloat16 [256, 2048], P('req')
Inputs may be any that keep to these rules, and one draw needn't show every extreme that they name: `lengths`: each device of req holds at most one request with more than 128 cached tokens; all others have 32 to 128; in every draw some request has exactly 1024. `page_table`: entry j of row r, for j below ceil(lengths[r] / 16), is the page (numbered within the home device r // 16) holding tokens j * 16 to (j + 1) * 16 - 1 of request r; no page serves two such entries; the entries after those are 183. dest_slot is a permutation. The request in slot k of device i of req (index i * 16 + k) goes to slot k of device (i + o_k) mod (16), with offsets o_k the same for all devices; at most 2 requests of one device go to one device, and exactly 2 do for some pairs.
All inputs are finite; a program needn't handle non-finite values.
Results may differ from a plain program's by a relative error of at most 0.01.
Values may be sent and summed in bfloat16 or wider, within the bound.
A program may use at most 64 MiB of HBM per device.

v0:
```python
import jax
import jax.numpy as jnp
from jax import lax
from jax.sharding import PartitionSpec as P


def normalize(values, scale_gain):
    wide = values.astype(jnp.float32)
    factor = lax.rsqrt(jnp.mean(wide * wide, axis=-1, keepdims=True) + 1e-05)
    return (wide * factor * scale_gain).astype(jnp.bfloat16)


def rotate(values, positions):
    half_size = values.shape[-1] // 2
    freqs = jnp.exp(
        -jnp.log(1000000.0) * 2.0 * jnp.arange(half_size, dtype=jnp.float32) / (2 * half_size)
    )
    angles = positions.astype(jnp.float32)[:, None, None] * freqs
    cosine = jnp.cos(angles)
    sine = jnp.sin(angles)
    first = values[..., :half_size]
    second = values[..., half_size:]
    return jnp.concatenate(
        [first * cosine - second * sine, second * cosine + first * sine], axis=-1
    )


def attend(query, new_key, new_value, page_pool, lengths, page_table):
    row_count = query.shape[0]
    group_size = query.shape[1]
    head_size = query.shape[2]
    page_count = page_pool.shape[0]
    page_size = page_pool.shape[1]
    table_width = page_table.shape[1]
    scale = 1.0 / jnp.sqrt(jnp.float32(head_size))
    used_pages = (lengths + page_size - 1) // page_size
    valid = jnp.arange(table_width, dtype=jnp.int32)[None, :] < used_pages[:, None]
    matches = (
        page_table[:, :, None] == jnp.arange(page_count, dtype=jnp.int32)[None, None, :]
    ) & valid[:, :, None]
    owner_int = jnp.sum(matches.astype(jnp.int32), axis=1)
    owner = owner_int.astype(jnp.float32)
    offsets = (jnp.arange(table_width, dtype=jnp.int32) * page_size)[None, :, None]
    page_base = jnp.sum(matches.astype(jnp.int32) * offsets, axis=(0, 1))
    page_limit = jnp.sum(owner_int * lengths[:, None], axis=0)
    live = (
        page_base[:, None] + jnp.arange(page_size, dtype=jnp.int32)[None, :] < page_limit[:, None]
    )
    page_query = jnp.dot(
        owner.T.astype(jnp.bfloat16),
        query.reshape(row_count, group_size * head_size),
        preferred_element_type=jnp.float32,
    )
    page_query = page_query.astype(jnp.bfloat16).reshape(page_count, group_size, head_size)
    scores = (
        jnp.einsum(
            "pjc,ptc->pjt",
            page_query,
            page_pool[:, :, :head_size],
            preferred_element_type=jnp.float32,
        )
        * scale
    )
    scores = jnp.where(live[:, None, :], scores, -jnp.inf)
    score_new = jnp.einsum("rjc,rc->rj", query, new_key, preferred_element_type=jnp.float32) * scale
    page_top = jnp.max(scores, axis=-1)
    row_top = jnp.max(jnp.where(owner_int[:, :, None] > 0, page_top[None, :, :], -jnp.inf), axis=1)
    row_top = jnp.maximum(row_top, score_new)
    spread_top = jnp.dot(owner.T, row_top, precision=lax.Precision.HIGHEST)
    weights = jnp.exp(scores - spread_top[:, :, None])
    weight_new = jnp.exp(score_new - row_top)
    total = jnp.dot(owner, jnp.sum(weights, axis=-1), precision=lax.Precision.HIGHEST) + weight_new
    page_sums = jnp.einsum(
        "pjt,ptc->pjc",
        weights.astype(jnp.bfloat16),
        page_pool[:, :, head_size:],
        preferred_element_type=jnp.float32,
    )
    numer = jnp.dot(
        owner,
        page_sums.reshape(page_count, group_size * head_size),
        precision=lax.Precision.HIGHEST,
    )
    numer = numer.reshape(row_count, group_size, head_size)
    numer = (
        numer
        + weight_new.astype(jnp.bfloat16).astype(jnp.float32)[:, :, None]
        * new_value.astype(jnp.float32)[:, None, :]
    )
    return (
        (numer / total[:, :, None]).astype(jnp.bfloat16).reshape(row_count, group_size * head_size)
    )


def relocate(mixed, dest_slot):
    row_count = mixed.shape[0]
    device_count = lax.axis_size("req")
    own_index = lax.axis_index("req")
    target_device = dest_slot // row_count
    shift_amount = (target_device - own_index) % device_count
    collected = lax.all_gather(mixed, "req", axis=0, tiled=True)
    source_device = (own_index - shift_amount) % device_count
    source_rows = source_device * row_count + jnp.arange(row_count, dtype=jnp.int32)
    return jnp.take(collected, source_rows, axis=0)


def local(state, norm_gain, w_qkv, w_out, kv_cache, lengths, page_table, dest_slot):
    row_count = state.shape[0]
    width = state.shape[1]
    head_size = kv_cache.shape[3] // 2
    group_size = w_out.shape[1] // head_size
    normed = normalize(state, norm_gain)
    proj = jnp.dot(normed, w_qkv.reshape(width, w_qkv.shape[2]), preferred_element_type=jnp.float32)
    query = rotate(
        proj[:, : group_size * head_size].reshape(row_count, group_size, head_size), lengths
    ).astype(jnp.bfloat16)
    new_key = rotate(proj[:, None, group_size * head_size : (group_size + 1) * head_size], lengths)[
        :, 0
    ].astype(jnp.bfloat16)
    new_value = proj[:, (group_size + 1) * head_size :].astype(jnp.bfloat16)
    attn = attend(query, new_key, new_value, kv_cache[:, 0], lengths, page_table)
    partial_out = jnp.dot(attn, w_out[0], preferred_element_type=jnp.float32)
    summed = lax.psum(partial_out, "tp")
    mixed = (state.astype(jnp.float32) + summed).astype(jnp.bfloat16)
    return relocate(mixed, dest_slot)


def solution(mesh):
    placed = (
        P("req", None),
        P(),
        P(None, "tp", None),
        P("tp", None, None),
        P("req", "tp", None, None),
        P("req"),
        P("req", None),
        P("req"),
    )
    return jax.shard_map(
        local, mesh=mesh, in_specs=placed, out_specs=P("req", None), check_vma=False
    )
```

profile of v0, /device:TPU:0, one launch (start us, length us, event | category | flops | bytes accessed | tf_op | source)
XLA Modules:
  0.0 92.7 jit_solution(18286603399373292580)
XLA Ops:
  6.5 0.0 copy-start
  6.5 0.0 all-reduce.2.cloned.1.call-start
  6.6 0.8 fusion.54
  7.4 0.1 iota_compare_fusion.1
  7.5 1.2 %select_reduce_fusion = (s32[184]{0:T(256)S(1)}, s32[16,184]{1,0:T(8,128)S(1)}) fusion(s32[64]{0:T(128)S(1)} %iota_multiply_fusion, s32[16,64]{1,0:T(8,128)} %param.14, pred[16,64]{1,0:T(8,128)(4,1)S(1)} %iota_compare_fusion.1), kind=kLoop, calls=%fused_computation.13 | loop fusion | flops 1127368 | bytes 17888 | tf_op jit(solution)/shard_map/reduce_sum | solution.py:44
  8.7 0.7 multiply_reduce_fusion
  9.4 1.0 %fusion.14 = f32[16]{0:T(128)S(1)} fusion(bf16[16,2048]{1,0:T(8,128)(2,1)} %param.8), kind=kLoop, calls=%fused_computation.27 | loop fusion | flops 98288 | bytes 65600 | tf_op jit(solution)/shard_map/reduce_sum | solution.py:9
  10.4 0.0 copy-done
  10.4 1.3 %fusion = f32[16,512]{1,0:T(8,128)S(1)} fusion(bf16[2048,1,512]{2,0,1:T(8,128)(2,1)S(1)} %copy-done, bf16[16,2048]{1,0:T(8,128)(2,1)} %param.8, f32[2048]{0:T(1024)} %param.9, f32[16]{0:T(128)S(1)} %add_rsqrt_fusion), kind=kOutput, calls=%fused_computation.1 | convolution fusion | flops 33685504 | bytes 2203712 | tf_op jit(solution)/shard_map/dot_general | solution.py:113
  11.7 0.1 multiply_cosine_fusion.1
  11.8 0.1 multiply_subtract_fusion
  11.9 0.1 maximum_convert_fusion
  12.0 0.2 convolution_convert_fusion
  12.3 0.1 add_compare_fusion
  12.4 1.7 %fusion.55 = (f32[184,2]{1,0:T(8,128)S(1)}, f32[184,2,16]{2,1,0:T(2,128)S(1)}) fusion(bf16[184,2,128]{2,1,0:T(2,128)(2,1)S(1)} %reshape.207, bf16[184,16,256]{2,1,0:T(8,128)(2,1)} %bitcast.55, pred[184,16]{1,0:T(8,128)(4,1)S(1)} %add_compare_fusion), kind=kOutput, calls=%fused_computation.105 | convolution fusion | flops 1524624 | bytes 875840 | tf_op jit(solution)/shard_map/pjc,ptc->pjt/dot_general | solution.py:56
  14.1 0.0 copy-start.1
  14.1 0.1 copy.16
  14.2 0.1 fusion.35
  14.3 0.1 maximum_bitcast_fusion
  14.4 0.1 fusion.42
  14.5 0.1 copy.21
  14.6 0.1 select_reduce_fusion.1
  14.7 0.4 fusion.28
  15.1 0.0 copy-start.2
  15.1 1.6 %fusion.9 = f32[184,2,128]{2,1,0:T(2,128)S(1)} fusion(bf16[184,16,256]{2,1,0:T(8,128)(2,1)} %bitcast.56, f32[184,2,16]{2,1,0:T(2,128)S(1)} %get-tuple-element.18, f32[184,2]{1,0:T(8,128)S(1)} %fusion.28), kind=kOutput, calls=%fused_computation.17 | convolution fusion | flops 1519104 | bytes 967104 | tf_op jit(solution)/shard_map/pjt,ptc->pjc/dot_general | solution.py:73
  16.7 0.0 copy-start.3
  16.7 0.5 fusion.18
  17.2 0.3 convolution_add_fusion.1
  17.5 0.2 fusion.5
  17.8 0.0 copy-done.1
  17.8 0.9 fusion.6
  18.7 0.0 all-reduce.2.cloned.1.call-update
  18.7 0.0 all-gather.2.cloned.1.call-start
  18.7 24.2 %all-reduce.2.cloned.1.call-done = f32[16,2048]{1,0:T(8,128)} async-done(((f32[16,2048]{1,0:T(8,128)}), f32[16,2048]{1,0:T(8,128)}) %all-reduce.2.cloned.1.call-update) | async-done | bytes 131088 | tf_op jit(solution)/shard_map/psum | solution.py:123
  43.0 0.0 copy-done.2
  43.0 1.5 %fusion.17 = bf16[16,2048]{1,0:T(8,128)(2,1)} fusion(f32[16,2048]{1,0:T(8,128)} %all-reduce.2.cloned.1.call-done, bf16[16,2048]{1,0:T(8,128)(2,1)S(1)} %copy-done.2), kind=kLoop, calls=%fused_computation.30 | loop fusion | flops 98304 | bytes 262144 | tf_op jit(solution)/shard_map/convert_element_type | solution.py:124
  44.5 0.0 all-gather.2.cloned.1.call-update
  44.6 0.0 copy-done.3
  44.6 38.5 %all-gather.2.cloned.1.call-done = bf16[256,2048]{1,0:T(8,128)(2,1)} async-done(((bf16[16,2048]{1,0:T(8,128)(2,1)}), bf16[256,2048]{1,0:T(8,128)(2,1)}) %all-gather.2.cloned.1.call-update) | async-done | bytes 1048592 | tf_op jit(solution)/shard_map/all_gather | solution.py:101
  83.1 2.0 %gather_fusion = bf16[16,2048]{1,0:T(8,128)(2,1)S(1)} fusion(bf16[256,2048]{1,0:T(8,128)(2,1)} %all-gather.2.cloned.1.call-done, s32[1024]{0:T(1024)S(1)} %pad_clamp_fusion), kind=kCustom, calls=%fused_computation | custom fusion | bytes 131136 | tf_op jit(solution)/shard_map/jit(_take)/gather | solution.py:104
  85.1 0.7 broadcast_select_fusion
  (12 shorter events, 0.1 us)
Async XLA Ops:
  6.5 3.9 %copy-start = (bf16[2048,1,512]{2,0,1:T(8,128)(2,1)S(1)}, bf16[2048,1,512]{2,0,1:T(8,128)(2,1)}, u32[]{:S(2)}) copy-start(bf16[2048,1,512]{2,0,1:T(8,128)(2,1)} %param.10) | copy-start | bytes 6291460
  6.5 36.4 %all-reduce.2.cloned.1.call-start = ((), (), s32[]{:S(2)}) async-start(), calls=%async_computation | async-start | bytes 262144 | tf_op jit(solution)/shard_map/psum | solution.py:123
  14.1 3.7 %copy-start.1 = (bf16[1,256,2048]{2,1,0:T(8,128)(2,1)S(1)}, bf16[1,256,2048]{2,1,0:T(8,128)(2,1)}, u32[]{:S(2)}) copy-start(bf16[1,256,2048]{2,1,0:T(8,128)(2,1)} %param.11) | copy-start | bytes 3145732
  15.1 27.9 %copy-start.2 = (bf16[16,2048]{1,0:T(8,128)(2,1)S(1)}, bf16[16,2048]{1,0:T(8,128)(2,1)}, u32[]{:S(2)}) copy-start(bf16[16,2048]{1,0:T(8,128)(2,1)} %param.8) | copy-start | bytes 196612
  16.7 27.9 %copy-start.3 = (s32[16]{0:T(128)S(1)}, s32[16]{0:T(128)}, u32[]{:S(2)}) copy-start(s32[16]{0:T(128)} %param.15) | copy-start | bytes 196
  18.7 64.4 %all-gather.2.cloned.1.call-start = ((), (), s32[]{:S(2)}) async-start(), calls=%async_computation.1 | async-start | bytes 1114112 | tf_op jit(solution)/shard_map/all_gather | solution.py:101
Sparse Core Ops, SparseCore 0:
  18.8 24.1 all-reduce.1
  45.1 37.9 all-gather.1
where the time goes:
time: 93.1 us; the launch traced here: 92.7 us
  waiting for transfers between devices  62.8 us (67%)
  between operations  13.6 us (15%)
  other arithmetic  7.4 us (8%)
  matrix products  6.65 us (7%)
  local copies, waits for them, and re-layouts  2.24 us (2%)
    all_gather x1, waiting for transfers between devices, relocate(): collected = lax.all_gather(mixed, 'req', axis=0, tiled=True)  38.5 us
    psum x1, waiting for transfers between devices, local(): summed = lax.psum(partial_out, 'tp')  24.2 us
    gather x1, local copies, waits for them, and re-layouts, relocate(): return jnp.take(collected, source_rows, axis=0)  2.02 us
  transfers between devices with their start and end apart: 2, of which 2 were waited for; matrix products, arithmetic and copies ran while one was open for 0% of the time, Pallas kernels for 0%

commit v1 on v0

--- a/solution.py
+++ b/solution.py
@@ -2,6 +2,12 @@
 import jax.numpy as jnp
 from jax import lax
 from jax.sharding import PartitionSpec as P
+
+
+def summed_here(x, axis):
+    blocks = lax.all_gather(x, axis, axis=0, tiled=False)
+    total = blocks.sum(axis=0)
+    return total
 
 
 def normalize(values, scale_gain):
@@ -120,7 +126,7 @@
     new_value = proj[:, (group_size + 1) * head_size :].astype(jnp.bfloat16)
     attn = attend(query, new_key, new_value, kv_cache[:, 0], lengths, page_table)
     partial_out = jnp.dot(attn, w_out[0], preferred_element_type=jnp.float32)
-    summed = lax.psum(partial_out, "tp")
+    summed = summed_here(partial_out, "tp")
     mixed = (state.astype(jnp.float32) + summed).astype(jnp.bfloat16)
     return relocate(mixed, dest_slot)
 

time: 93.1 us -> 75.3 us (0.81)
  waiting for transfers between devices: 62.8 us -> 39.5 us
  blocking collectives: 0 us -> 7.11 us
    psum x1 -> x0, waiting for transfers between devices: 24.2 us -> none  [local(): summed = lax.psum(partial_out, 'tp')]
    all_gather x0 -> x1, blocking collectives: none -> 7.11 us  [summed_here(): blocks = lax.all_gather(x, axis, axis=0, tiled=False)]
    all_gather x1, waiting for transfers between devices: 38.5 us -> 39.5 us  [relocate(): collected = lax.all_gather(mixed, 'req', axis=0, tiled=True)]
  transfers between devices with their start and end apart: 2 -> 1, of which waited for: 2 -> 1; matrix products, arithmetic and copies ran while one was open for 0% -> 0% of each run, Pallas kernels for 0% -> 0%
where the time goes in v1:
time: 75.3 us; the launch traced here: 75 us
  waiting for transfers between devices  39.5 us (52%)
  between operations  13.6 us (18%)
  blocking collectives  7.11 us (9%)
  other arithmetic  6.51 us (9%)
  matrix products  5.97 us (8%)
  local copies, waits for them, and re-layouts  2.24 us (3%)
    all_gather x1, waiting for transfers between devices, relocate(): collected = lax.all_gather(mixed, 'req', axis=0, tiled=True)  39.5 us
    all_gather x1, blocking collectives, summed_here(): blocks = lax.all_gather(x, axis, axis=0, tiled=False)  7.11 us
    gather x1, local copies, waits for them, and re-layouts, relocate(): return jnp.take(collected, source_rows, axis=0)  2.02 us
    dot_general x1, matrix products, attend(): jnp.einsum('pjc,ptc->pjt', page_query, page_pool[:, :, :head_size], prefe...  1.71 us
    dot_general x1, matrix products, attend(): jnp.einsum('pjt,ptc->pjc', weights.astype(jnp.bfloat16), page_pool[:, :,...  1.54 us
  transfers between devices with their start and end apart: 1, of which 1 were waited for; matrix products, arithmetic and copies ran while one was open for 0% of the time, Pallas kernels for 0%

profile of v1, /device:TPU:0, one launch (start us, length us, event | category | flops | bytes accessed | tf_op | source)
XLA Modules:
  0.0 75.0 jit_solution(329618740508900567)
XLA Ops:
  6.5 0.0 copy-start
  6.5 0.0 all-gather.3.cloned.1.call-start
  6.6 0.8 %fusion.54 = (f32[16]{0:T(128)S(1)}, s32[16]{0:T(128)S(1)}) fusion(s32[16]{0:T(128)} %param.13), kind=kLoop, calls=%fused_computation.104 | loop fusion | flops 272 | bytes 192 | tf_op jit(solution)/shard_map/convert_element_type | solution.py:24
  7.4 0.1 iota_compare_fusion.1
  7.5 1.2 %select_reduce_fusion = (s32[184]{0:T(256)S(1)}, s32[16,184]{1,0:T(8,128)S(1)}) fusion(s32[64]{0:T(128)S(1)} %iota_multiply_fusion, s32[16,64]{1,0:T(8,128)} %param.14, pred[16,64]{1,0:T(8,128)(4,1)S(1)} %iota_compare_fusion.1), kind=kLoop, calls=%fused_computation.13 | loop fusion | flops 1127368 | bytes 17888 | tf_op jit(solution)/shard_map/reduce_sum | solution.py:50
  8.7 0.7 multiply_reduce_fusion
  9.4 1.0 %fusion.14 = f32[16]{0:T(128)S(1)} fusion(bf16[16,2048]{1,0:T(8,128)(2,1)} %param.8), kind=kLoop, calls=%fused_computation.27 | loop fusion | flops 98288 | bytes 65600 | tf_op jit(solution)/shard_map/reduce_sum | solution.py:15
  10.4 0.0 copy-done
  10.4 1.3 %fusion = f32[16,512]{1,0:T(8,128)S(1)} fusion(bf16[2048,1,512]{2,0,1:T(8,128)(2,1)S(1)} %copy-done, bf16[16,2048]{1,0:T(8,128)(2,1)} %param.8, f32[2048]{0:T(1024)} %param.9, f32[16]{0:T(128)S(1)} %add_rsqrt_fusion), kind=kOutput, calls=%fused_computation.1 | convolution fusion | flops 33685504 | bytes 2203712 | tf_op jit(solution)/shard_map/dot_general | solution.py:119
  11.7 0.1 multiply_cosine_fusion.1
  11.8 0.1 multiply_subtract_fusion
  11.9 0.1 maximum_convert_fusion
  12.0 0.2 convolution_convert_fusion
  12.3 0.1 add_compare_fusion
  12.4 1.7 %fusion.55 = (f32[184,2]{1,0:T(8,128)S(1)}, f32[184,2,16]{2,1,0:T(2,128)S(1)}) fusion(bf16[184,2,128]{2,1,0:T(2,128)(2,1)S(1)} %reshape.207, bf16[184,16,256]{2,1,0:T(8,128)(2,1)} %bitcast.57, pred[184,16]{1,0:T(8,128)(4,1)S(1)} %add_compare_fusion), kind=kOutput, calls=%fused_computation.105 | convolution fusion | flops 1524624 | bytes 875840 | tf_op jit(solution)/shard_map/pjc,ptc->pjt/dot_general | solution.py:62
  14.1 0.0 copy-start.1
  14.1 0.1 copy.16
  14.2 0.1 fusion.35
  14.3 0.1 maximum_bitcast_fusion
  14.4 0.1 fusion.42
  14.5 0.1 copy.21
  14.6 0.1 select_reduce_fusion.1
  14.7 0.4 fusion.28
  15.1 1.5 %fusion.9 = f32[184,2,128]{2,1,0:T(2,128)S(1)} fusion(bf16[184,16,256]{2,1,0:T(8,128)(2,1)} %bitcast.58, f32[184,2,16]{2,1,0:T(2,128)S(1)} %get-tuple-element.18, f32[184,2]{1,0:T(8,128)S(1)} %fusion.28), kind=kOutput, calls=%fused_computation.17 | convolution fusion | flops 1519104 | bytes 967104 | tf_op jit(solution)/shard_map/pjt,ptc->pjc/dot_general | solution.py:79
  16.6 0.0 copy-start.2
  16.7 0.0 copy-start.3
  16.7 0.5 fusion.18
  17.2 0.3 convolution_add_fusion.1
  17.5 0.2 fusion.5
  17.7 0.0 copy-done.1
  17.7 0.3 fusion.6
  18.0 7.1 %all-gather = f32[32,2048]{1,0:T(8,128)S(1)} all-gather(f32[16,2048]{1,0:T(8,128)S(1)} %fusion.6), channel_id=2, replica_groups=mesh['req'=16,'tp'=2] {'tp'}, dimensions={0}, use_global_device_ids=true | all-gather | bytes 393216 | tf_op jit(solution)/shard_map/all_gather | solution.py:8
  25.1 0.0 copy-done.2
  25.1 0.6 fusion.17
  25.8 0.0 all-gather.3.cloned.1.call-update
  25.8 0.0 copy-done.3
  25.9 39.5 %all-gather.3.cloned.1.call-done = bf16[256,2048]{1,0:T(8,128)(2,1)} async-done(((bf16[16,2048]{1,0:T(8,128)(2,1)}), bf16[256,2048]{1,0:T(8,128)(2,1)}) %all-gather.3.cloned.1.call-update) | async-done | bytes 1048592 | tf_op jit(solution)/shard_map/all_gather | solution.py:107
  65.4 2.0 %gather_fusion = bf16[16,2048]{1,0:T(8,128)(2,1)S(1)} fusion(bf16[256,2048]{1,0:T(8,128)(2,1)} %all-gather.3.cloned.1.call-done, s32[1024]{0:T(1024)S(1)} %pad_clamp_fusion), kind=kCustom, calls=%fused_computation | custom fusion | bytes 131136 | tf_op jit(solution)/shard_map/jit(_take)/gather | solution.py:110
  67.4 0.7 broadcast_select_fusion
  (13 shorter events, 0.1 us)
Async XLA Ops:
  6.5 3.9 %copy-start = (bf16[2048,1,512]{2,0,1:T(8,128)(2,1)S(1)}, bf16[2048,1,512]{2,0,1:T(8,128)(2,1)}, u32[]{:S(2)}) copy-start(bf16[2048,1,512]{2,0,1:T(8,128)(2,1)} %param.10) | copy-start | bytes 6291460
  6.5 58.9 %all-gather.3.cloned.1.call-start = ((), (), s32[]{:S(2)}) async-start(), calls=%async_computation | async-start | bytes 1114112 | tf_op jit(solution)/shard_map/all_gather | solution.py:107
  14.1 3.6 %copy-start.1 = (bf16[1,256,2048]{2,1,0:T(8,128)(2,1)S(1)}, bf16[1,256,2048]{2,1,0:T(8,128)(2,1)}, u32[]{:S(2)}) copy-start(bf16[1,256,2048]{2,1,0:T(8,128)(2,1)} %param.11) | copy-start | bytes 3145732
  16.6 8.5 %copy-start.2 = (bf16[16,2048]{1,0:T(8,128)(2,1)S(1)}, bf16[16,2048]{1,0:T(8,128)(2,1)}, u32[]{:S(2)}) copy-start(bf16[16,2048]{1,0:T(8,128)(2,1)} %param.8) | copy-start | bytes 196612
  16.7 9.2 %copy-start.3 = (s32[16]{0:T(128)S(1)}, s32[16]{0:T(128)}, u32[]{:S(2)}) copy-start(s32[16]{0:T(128)} %param.15) | copy-start | bytes 196
Sparse Core Ops, SparseCore 0:
  25.9 39.4 all-gather.2
